TPU v7x, 32 devices: a whole 2x2x4 slice. The times are simulated.
32 devices in a mesh: rep: 4 (over y, x), shard: 8 (over z, core).
Axes of the slice: x: 2, y: 2, z: 4, core: 2. Of those that a mesh axis runs over, the one named last changes fastest.
Arguments:
- inputs: bfloat16 [32768, 1024], P(('rep', 'shard')), may hold values from -6 to 6
- query_weight: bfloat16 [1024, 256], P('shard'), may hold values from -0.1875 to 0.1875
- key_weight: bfloat16 [1024, 256], P('shard'), may hold values from -0.1875 to 0.1875
- value_weight: bfloat16 [1024, 1024], P('shard'), may hold values from -0.1875 to 0.1875
- out_weight: bfloat16 [1024, 1024], P('shard'), may hold values from -6 to 6
- gate_weight: bfloat16 [1024, 2752], P('shard'), may hold values from -0.1875 to 0.1875
- up_weight: bfloat16 [1024, 2752], P('shard'), may hold values from -0.1875 to 0.1875
- down_weight: bfloat16 [1024, 2752], P('shard'), may hold values from -0.109375 to 0.109375
- attn_gain: bfloat16 [1024], P('shard'), may hold values from 0.25 to 1.75
- mlp_gain: bfloat16 [1024], P('shard'), may hold values from 0.25 to 1.75
- slot_of: int32 [4, 8], P('rep'), may hold values from 0 to 7, each once within a row
- parent_of: int32 [4, 8], P('rep'), may hold values from 0 to 1, as said below
- cotangent: bfloat16 [32768, 1024], P(('rep', 'shard')), may hold values from -6 to 6
Outputs:
- block_out: bfloat16 [32768, 1024], P(('rep', 'shard'))
- input_grad: float32 [32768, 1024], P(('rep', 'shard'))
- query_grad: float32 [1024, 256], P('shard')
- key_grad: float32 [1024, 256], P('shard')
- value_grad: float32 [1024, 1024], P('shard')
- out_grad: float32 [1024, 1024], P('shard')
- gate_grad: float32 [1024, 2752], P('shard')
- up_grad: float32 [1024, 2752], P('shard')
- down_grad: float32 [1024, 2752], P('shard')
- attn_gain_grad: float32 [1024], P('shard')
- mlp_gain_grad: float32 [1024], P('shard')
Inputs may be any that keep to these rules, and one draw needn't show every extreme that they name: `slot_of`: each row is a permutation of the slots of its group. `parent_of`: each row names each of the 2 families for exactly 4 continuations.
All inputs are finite; a program needn't handle non-finite values.
Results may differ from a plain program's by a relative error of at most 0.02.
Values may be sent and summed in bfloat16 or wider, within the bound.
No kernel may reach another device: no remote copies, remote signals or barrier semaphores. Data moves between devices by JAX's collectives and lax.ppermute only.
A program may use at most 320 MiB of HBM per device.

v0:
```python
from functools import partial
import math
import jax
import jax.numpy as jnp
from jax import lax
from jax.sharding import PartitionSpec as P

HEADS = 16
CONT_PER = 4
norm_eps = 1e-05


def on_whole(value, axis, dim, block):
    whole = lax.all_gather(value, axis, axis=dim, tiled=True)
    return block(whole, jnp.int32(0))


def features(vectors):
    width = vectors.shape[-1]
    square = vectors[..., :, None] * vectors[..., None, :]
    square = square.reshape(vectors.shape[:-1] + (width * width,))
    return jnp.concatenate(
        [
            jnp.ones_like(vectors[..., :1]),
            vectors / width**0.25,
            square / (math.sqrt(2.0) * math.sqrt(width)),
        ],
        axis=-1,
    )


def contract_last(left, right):
    return lax.dot_general(
        left, right, (((1,), (1,)), ((), ())), preferred_element_type=jnp.float32
    )


def contract_first(left, right):
    return lax.dot_general(
        left, right, (((0,), (0,)), ((), ())), preferred_element_type=jnp.float32
    )


def group_heads(values):
    rows_count, heads_count, inner_dim = values.shape
    return values.reshape(rows_count, heads_count // 4, 4, inner_dim).transpose(1, 0, 2, 3)


def group_plain(values):
    rows_count, heads_count = values.shape
    return values.reshape(rows_count, heads_count // 4, 4).transpose(1, 0, 2)


def ungroup_heads(values):
    block_count, rows_count, block_heads, inner_dim = values.shape
    return values.transpose(1, 0, 2, 3).reshape(rows_count, block_count * block_heads, inner_dim)


def ungroup_plain(values):
    block_count, rows_count, block_heads = values.shape
    return values.transpose(1, 0, 2).reshape(rows_count, block_count * block_heads)


def kernel_of(queries, key_heads, allowed):
    scores = jnp.einsum(
        "thf,uhf->htu", queries, key_heads, preferred_element_type=jnp.float32
    ) / math.sqrt(queries.shape[-1])
    kernel = jnp.where(allowed[None], 1.0 + scores + 0.5 * scores * scores, 0.0)
    return (scores, kernel)


def local_forward(allowed, blocks):
    queries, key_heads, value_heads = blocks
    scores, kernel = kernel_of(queries, key_heads, allowed)
    numerator = jnp.einsum(
        "htu,uhe->the", kernel.astype(jnp.bfloat16), value_heads, preferred_element_type=jnp.float32
    )
    denominator = jnp.sum(kernel, axis=2).T
    return (numerator, denominator)


def local_backward(allowed, blocks):
    queries, key_heads, value_heads, grad_num, grad_den = blocks
    scores, kernel = kernel_of(queries, key_heads, allowed)
    grad_kernel = (
        jnp.einsum("the,uhe->htu", grad_num, value_heads, preferred_element_type=jnp.float32)
        + grad_den.T.astype(jnp.float32)[:, :, None]
    )
    grad_scores = (jnp.where(allowed[None], grad_kernel, 0.0) * (1.0 + scores)).astype(jnp.bfloat16)
    root = math.sqrt(queries.shape[-1])
    grad_query = (
        jnp.einsum("htu,uhf->thf", grad_scores, key_heads, preferred_element_type=jnp.float32)
        / root
    )
    grad_key = (
        jnp.einsum("htu,thf->uhf", grad_scores, queries, preferred_element_type=jnp.float32) / root
    )
    grad_value = jnp.einsum(
        "htu,the->uhe", kernel.astype(jnp.bfloat16), grad_num, preferred_element_type=jnp.float32
    )
    return (grad_query, grad_key, grad_value)


def local(
    inputs,
    query_weight,
    key_weight,
    value_weight,
    out_weight,
    gate_weight,
    up_weight,
    down_weight,
    attn_gain,
    mlp_gain,
    slot_of,
    parent_of,
    cotangent,
):
    tok_rows, width = inputs.shape
    half_rows = tok_rows // 2
    qk_width = query_weight.shape[1]
    value_width = value_weight.shape[1]
    hidden_width = gate_weight.shape[1]
    state_rows = value_width + HEADS
    shards = lax.axis_size("shard")
    own_index = lax.axis_index("shard")
    slot_ids = slot_of[0]
    parent_ids = parent_of[0]
    prompt_slots = shards // 2
    pieces_per = CONT_PER // 2
    own_slot = lax.dynamic_index_in_dim(slot_ids, own_index, keepdims=False)
    own_prompt = own_slot < prompt_slots
    source_prompt = slot_ids < prompt_slots
    source_family = slot_ids // pieces_per
    earlier = (
        source_prompt
        & (source_family == own_slot // pieces_per)
        & (slot_ids % pieces_per < own_slot % pieces_per)
    )
    pair_index = jnp.clip(own_slot - prompt_slots, 0, shards // 2 - 1)
    first_parent = lax.dynamic_index_in_dim(parent_ids, 2 * pair_index, keepdims=False)
    second_parent = lax.dynamic_index_in_dim(parent_ids, 2 * pair_index + 1, keepdims=False)
    from_first = source_prompt & (source_family == first_parent)
    from_second = source_prompt & (source_family == second_parent)
    source_mix = jnp.where(
        own_prompt, jnp.stack([earlier, earlier]), jnp.stack([from_first, from_second])
    ).astype(jnp.float32)
    positions = lax.broadcasted_iota(jnp.int32, (tok_rows,), 0)
    segment_ids = jnp.where(own_prompt, 0, positions // half_rows)
    allowed = (positions[None, :] <= positions[:, None]) & (
        segment_ids[None, :] == segment_ids[:, None]
    )
    x_float = inputs.astype(jnp.float32)
    inv_one = lax.rsqrt(jnp.mean(x_float * x_float, axis=1, keepdims=True) + norm_eps)
    norm_one = x_float * inv_one
    part_query = lax.all_gather(query_weight, "shard", axis=0, tiled=True)
    part_key = lax.all_gather(key_weight, "shard", axis=0, tiled=True)
    part_value = lax.all_gather(value_weight, "shard", axis=0, tiled=True)
    part_gain = lax.all_gather(attn_gain, "shard", axis=0, tiled=True)
    scaled = (norm_one * part_gain.astype(jnp.float32)).astype(jnp.bfloat16)
    acc_query = jnp.dot(scaled, part_query, preferred_element_type=jnp.float32)
    acc_key = jnp.dot(scaled, part_key, preferred_element_type=jnp.float32)
    acc_value = jnp.dot(scaled, part_value, preferred_element_type=jnp.float32)
    hidden_one = scaled
    gain_one = part_gain
    queries = acc_query.astype(jnp.bfloat16).reshape(tok_rows, HEADS, -1)
    key_heads = acc_key.astype(jnp.bfloat16).reshape(tok_rows, HEADS, -1)
    value_heads = acc_value.astype(jnp.bfloat16).reshape(tok_rows, HEADS, -1)
    query_float = queries.astype(jnp.float32)
    key_float = key_heads.astype(jnp.float32)
    query_feat = features(query_float).astype(jnp.bfloat16)
    key_feat = features(key_float).astype(jnp.bfloat16)
    taylor = query_feat.shape[2]
    ones_col = jnp.ones((tok_rows,), jnp.bfloat16)
    value_state = jnp.einsum(
        "the,thf->hef", value_heads, key_feat, preferred_element_type=jnp.float32
    ).reshape(value_width, taylor)
    norm_state = jnp.einsum("t,thf->hf", ones_col, key_feat, preferred_element_type=jnp.float32)
    own_state = jnp.concatenate([value_state, norm_state], axis=0).astype(jnp.bfloat16)
    add_portion = lax.all_gather(own_state, "shard", axis=0, tiled=True)
    sources = add_portion.shape[0] // state_rows
    mix = source_mix.astype(jnp.bfloat16)
    slot_states = jnp.einsum(
        "sn,nrf->srf",
        mix,
        add_portion.reshape(sources, state_rows, taylor),
        preferred_element_type=jnp.float32,
    )
    used_states = slot_states.astype(jnp.bfloat16)
    used_values = used_states[:, :value_width].reshape(2, HEADS, -1, taylor)
    used_norms = used_states[:, value_width:]
    halves_query = query_feat.reshape(2, half_rows, HEADS, taylor)
    state_num = jnp.einsum(
        "nthf,nhef->nthe", halves_query, used_values, preferred_element_type=jnp.float32
    ).reshape(tok_rows, HEADS, -1)
    state_den = jnp.einsum(
        "nthf,nhf->nth", halves_query, used_norms, preferred_element_type=jnp.float32
    ).reshape(tok_rows, HEADS)
    local_num, local_den = lax.map(
        partial(local_forward, allowed),
        (group_heads(queries), group_heads(key_heads), group_heads(value_heads)),
    )
    numerator = ungroup_heads(local_num) + state_num
    denominator = ungroup_plain(local_den) + state_den
    ratio = numerator / denominator[:, :, None]
    mixed = ratio.reshape(tok_rows, value_width).astype(jnp.bfloat16)
    attn_out = on_whole(
        out_weight, "shard", 0, lambda portion, offset: contract_last(mixed, portion)
    )
    after_attn = x_float + attn_out
    inv_two = lax.rsqrt(jnp.mean(after_attn * after_attn, axis=1, keepdims=True) + norm_eps)
    norm_two = after_attn * inv_two
    part_gate = lax.all_gather(gate_weight, "shard", axis=0, tiled=True)
    part_up = lax.all_gather(up_weight, "shard", axis=0, tiled=True)
    part_gain = lax.all_gather(mlp_gain, "shard", axis=0, tiled=True)
    scaled = (norm_two * part_gain.astype(jnp.float32)).astype(jnp.bfloat16)
    gate_pre = jnp.dot(scaled, part_gate, preferred_element_type=jnp.float32)
    up_pre = jnp.dot(scaled, part_up, preferred_element_type=jnp.float32)
    sigma = jax.nn.sigmoid(gate_pre)
    activated = (gate_pre * sigma * up_pre).astype(jnp.bfloat16)
    mlp_out = on_whole(
        down_weight, "shard", 0, lambda portion, offset: contract_last(activated, portion)
    )
    block_out = (after_attn + mlp_out).astype(jnp.bfloat16)
    cot_float = cotangent.astype(jnp.float32)
    grad_act = jnp.dot(
        cotangent,
        lax.all_gather(down_weight, "shard", axis=0, tiled=True),
        preferred_element_type=jnp.float32,
    )
    grad_up = (grad_act * gate_pre * sigma).astype(jnp.bfloat16)
    grad_gate = (grad_act * up_pre * sigma * (1.0 + gate_pre * (1.0 - sigma))).astype(jnp.bfloat16)
    grad_hidden_two = on_whole(
        (gate_weight, up_weight),
        "shard",
        0,
        lambda portion, offset: contract_last(grad_gate, portion[0])
        + contract_last(grad_up, portion[1]),
    )
    grad_norm_two = grad_hidden_two * part_gain.astype(jnp.float32)
    grad_after = cot_float + inv_two * (
        grad_norm_two - norm_two * jnp.mean(grad_norm_two * norm_two, axis=1, keepdims=True)
    )
    grad_attn = grad_after.astype(jnp.bfloat16)
    grad_mixed = jnp.dot(
        grad_attn,
        lax.all_gather(out_weight, "shard", axis=0, tiled=True),
        preferred_element_type=jnp.float32,
    ).reshape(tok_rows, HEADS, -1)
    grad_num = (grad_mixed / denominator[:, :, None]).astype(jnp.bfloat16)
    grad_den = (-jnp.sum(grad_mixed * ratio, axis=2) / denominator).astype(jnp.bfloat16)
    local_dq, local_dk, local_dv = lax.map(
        partial(local_backward, allowed),
        (
            group_heads(queries),
            group_heads(key_heads),
            group_heads(value_heads),
            group_heads(grad_num),
            group_plain(grad_den),
        ),
    )
    halves_num = grad_num.reshape(2, half_rows, HEADS, -1)
    halves_den = grad_den.reshape(2, half_rows, HEADS)
    grad_query_feat = (
        jnp.einsum("nthe,nhef->nthf", halves_num, used_values, preferred_element_type=jnp.float32)
        + jnp.einsum("nth,nhf->nthf", halves_den, used_norms, preferred_element_type=jnp.float32)
    ).reshape(tok_rows, HEADS, taylor)
    grad_slot_values = jnp.einsum(
        "nthf,nthe->nhef", halves_query, halves_num, preferred_element_type=jnp.float32
    ).reshape(2, value_width, taylor)
    grad_slot_norms = jnp.einsum(
        "nthf,nth->nhf", halves_query, halves_den, preferred_element_type=jnp.float32
    )
    grad_slots = jnp.concatenate([grad_slot_values, grad_slot_norms], axis=1)
    mix = source_mix
    grad_state = lax.psum_scatter(
        jnp.einsum("sn,srf->nrf", mix, grad_slots, precision=lax.Precision.HIGHEST)
        .reshape(state_rows * lax.axis_size("shard"), taylor)
        .astype(jnp.bfloat16),
        "shard",
        scatter_dimension=0,
        tiled=True,
    )
    grad_value_state = grad_state[:value_width].reshape(HEADS, -1, taylor)
    grad_norm_state = grad_state[value_width:]
    grad_key_feat = (
        jnp.einsum(
            "hef,the->thf", grad_value_state, value_heads, preferred_element_type=jnp.float32
        )
        + grad_norm_state.astype(jnp.float32)[None]
    )
    value_from_state = jnp.einsum(
        "thf,hef->the", key_feat, grad_value_state, preferred_element_type=jnp.float32
    )
    query_from_feat = jax.vjp(features, query_float)[1](grad_query_feat)[0]
    key_from_feat = jax.vjp(features, key_float)[1](grad_key_feat)[0]
    grad_queries = (
        (ungroup_heads(local_dq) + query_from_feat).reshape(tok_rows, qk_width).astype(jnp.bfloat16)
    )
    grad_keys = (
        (ungroup_heads(local_dk) + key_from_feat).reshape(tok_rows, qk_width).astype(jnp.bfloat16)
    )
    grad_values = (
        (ungroup_heads(local_dv) + value_from_state)
        .reshape(tok_rows, value_width)
        .astype(jnp.bfloat16)
    )
    grad_hidden_one = on_whole(
        (query_weight, key_weight, value_weight),
        "shard",
        0,
        lambda portion, offset: contract_last(grad_queries, portion[0])
        + contract_last(grad_keys, portion[1])
        + contract_last(grad_values, portion[2]),
    )
    grad_norm_one = grad_hidden_one * gain_one.astype(jnp.float32)
    input_grad = grad_after + inv_one * (
        grad_norm_one - norm_one * jnp.mean(grad_norm_one * norm_one, axis=1, keepdims=True)
    )
    gain_term_one = grad_hidden_one * norm_one
    gain_term_two = grad_hidden_two * norm_two
    grad_qkv = jnp.concatenate([grad_queries, grad_keys, grad_values], axis=1)
    grad_gate_up = jnp.concatenate([grad_gate, grad_up], axis=1)
    pick = lambda source_array: source_array
    group_share = lax.psum_scatter(
        jnp.concatenate(
            [
                contract_first(pick(hidden_one), grad_qkv),
                contract_first(pick(grad_attn), mixed),
                contract_first(pick(scaled), grad_gate_up),
                contract_first(pick(cotangent), activated),
                jnp.sum(pick(gain_term_one), axis=0)[:, None],
                jnp.sum(pick(gain_term_two), axis=0)[:, None],
            ],
            axis=1,
        ).astype(jnp.bfloat16),
        "shard",
        scatter_dimension=0,
        tiled=True,
    )
    own_grads = lax.psum(group_share, "rep").astype(jnp.float32)
    edge_two = qk_width + qk_width
    edge_three = edge_two + value_width
    edge_four = edge_three + value_width
    edge_five = edge_four + hidden_width
    edge_six = edge_five + hidden_width
    edge_seven = edge_six + hidden_width
    return (
        block_out,
        input_grad,
        own_grads[:, :qk_width],
        own_grads[:, qk_width:edge_two],
        own_grads[:, edge_two:edge_three],
        own_grads[:, edge_three:edge_four],
        own_grads[:, edge_four:edge_five],
        own_grads[:, edge_five:edge_six],
        own_grads[:, edge_six:edge_seven],
        own_grads[:, edge_seven],
        own_grads[:, edge_seven + 1],
    )


def solution(mesh):
    placed = (
        P(("rep", "shard"), None),
        P("shard", None),
        P("shard", None),
        P("shard", None),
        P("shard", None),
        P("shard", None),
        P("shard", None),
        P("shard", None),
        P("shard"),
        P("shard"),
        P("rep", None),
        P("rep", None),
        P(("rep", "shard"), None),
    )
    return jax.shard_map(
        local,
        mesh=mesh,
        in_specs=placed,
        out_specs=(
            P(("rep", "shard"), None),
            P(("rep", "shard"), None),
            P("shard", None),
            P("shard", None),
            P("shard", None),
            P("shard", None),
            P("shard", None),
            P("shard", None),
            P("shard", None),
            P("shard"),
            P("shard"),
        ),
        check_vma=False,
    )
```

profile of v0, /device:TPU:0, one launch (start us, length us, event | category | flops | bytes accessed | tf_op | source)
XLA Modules:
  0.0 1114.8 jit_solution(6212220869168196635)
XLA Ops:
  10.9 13.5 %all-gather = bf16[8,1,128]{2,1,0:T(2,128)(2,1)S(1)} all-gather(bf16[1,1,128]{2,1,0:T(2,128)(2,1)S(1)} %bitcast.339), channel_id=1, replica_groups=mesh['rep'=4,'shard'=8] {'shard'}, dimensions={0}, use_global_device_ids=true | all-gather | bytes 2304 | tf_op jit(solution)/shard_map/all_gather | solution.py:159
  24.9 17.3 %all_gather.40 = bf16[1024,256]{1,0:T(8,128)(2,1)S(1)} all-gather(bf16[128,256]{1,0:T(8,128)(2,1)S(1)} %copy-done.35), channel_id=1, replica_groups=mesh['rep'=4,'shard'=8] {'shard'}, dimensions={0}, use_global_device_ids=true | all-gather | bytes 589824 | tf_op jit(solution)/shard_map/all_gather | solution.py:157
  43.2 5.8 multiply_convert_fusion.2
  48.9 5.5 fusion.107
  74.0 17.6 %all_gather.39 = bf16[1024,256]{1,0:T(8,128)(2,1)S(1)} all-gather(bf16[128,256]{1,0:T(8,128)(2,1)S(1)} %copy-done.36), channel_id=1, replica_groups=mesh['rep'=4,'shard'=8] {'shard'}, dimensions={0}, use_global_device_ids=true | all-gather | bytes 589824 | tf_op jit(solution)/shard_map/all_gather | solution.py:156
  94.5 5.7 multiply_convert_fusion.1
  100.2 14.6 %div.136 = bf16[2,512,16,256]{1,0,3,2:T(2,128)(2,1)} reshape(bf16[1024,16,16,16]{0,3,2,1:T(8,128)(2,1)} %multiply_convert_fusion.1) | data formatting | bytes 16777216 | tf_op jit(solution)/shard_map/div | solution.py:26
  114.8 8.6 copy.125
  127.5 9.4 all-gather.2
  140.9 11.8 %pad_maximum_fusion.1 = bf16[2,512,16,273]{1,3,2,0:T(8,128)(2,1)} fusion(bf16[2,512,16,256]{1,3,2,0:T(8,128)(2,1)} %copy.125, bf16[2,512,16,16]{1,3,2,0:T(8,128)(2,1)} %copy.124, bf16[273]{0:T(512)(128)(2,1)S(1)} %pad.12.clone), kind=kLoop, calls=%fused_computation.76 | loop fusion | flops 26836992 | bytes 17859106 | tf_op jit(solution)/shard_map/concatenate | solution.py:22
  156.0 41.7 %while.32 = (s32[]{:T(128)}, f32[4,1024,4,64]{1,3,2,0:T(8,128)}, f32[4,1024,4]{1,2,0:T(4,128)S(1)}, bf16[4,1024,4,64]{1,3,2,0:T(8,128)(2,1)}, bf16[4,1024,4,16]{...) while((s32[]{:T(128)}, f32[4,1024,4,64]{1,3,2,0:T(8,128)}, ...), condition=%wide.region_3.4_spmd.clone, body=%wide.region_1.3_spmd.clone.sunk | while | flops 707784704 | bytes 20764768 | solution.py:199
  156.6 6.2 fusion.196
  167.0 6.2 fusion.196
  177.4 6.2 fusion.196
  187.8 6.2 fusion.196
  209.5 6.7 fusion.127
  235.5 11.5 %fusion.129 = f32[1024,2752]{0,1:T(8,128)} fusion(bf16[1024,2752]{0,1:T(8,128)(2,1)} %all-gather.14.cloned.1.call-done, bf16[1024,1024]{0,1:T(8,128)(2,1)S(1)} %multiply_convert_fusion.6), kind=kOutput, calls=%fused_computation.207 | convolution fusion | flops 5771362304 | bytes 19005440 | tf_op jit(solution)/shard_map/dot_general | solution.py:217
  247.0 26.2 %all-gather.16.cloned.1.call-done = bf16[1024,2752]{0,1:T(8,128)(2,1)} async-done(((bf16[128,2752]{0,1:T(8,128)(2,1)}), bf16[1024,2752]{0,1:T(8,128)(2,1)}) %all-gather.16.cloned.1.call-update) | async-done | bytes 5636112 | tf_op jit(solution)/shard_map/all_gather | solution.py:214
  273.2 11.1 fusion.130
  284.3 48.3 %all-gather.18.cloned.1.call-done = bf16[1024,2752]{0,1:T(8,128)(2,1)} async-done(((bf16[128,2752]{0,1:T(8,128)(2,1)}), bf16[1024,2752]{0,1:T(8,128)(2,1)}) %all-gather.18.cloned.1.call-update) | async-done | bytes 5636112 | tf_op jit(solution)/shard_map/all_gather | solution.py:14
  332.6 20.0 %multiply_convert_fusion.3 = (bf16[1024,2752]{0,1:T(8,128)(2,1)}, bf16[1024,2752]{0,1:T(8,128)(2,1)}, bf16[1024,2752]{0,1:T(8,128)(2,1)}) fusion(f32[1024,2752]{0,1:T(8,128)} %fusion.129, f32[1024,2752]{0,1:T(8,128)} %fusion.130, bf16[1024,1024]{1,0:T(8,128)(2,1)S(1)} %copy-done.25, bf16[1024,2752]{0,1:T(8,128)(2,1)} %all-gather.18.cloned.1.call-done), kind=kOutput, calls=%fused_computation.71 | convolution fusion | flops 5816451072 | bytes 47185920 | tf_op jit(solution)/shard_map/dot_general | solution.py:226
  352.6 11.3 %fusion.128 = f32[1024,1024]{0,1:T(8,128)} fusion(bf16[1024,2752]{0,1:T(8,128)(2,1)} %get-tuple-element.371, bf16[1024,2752]{0,1:T(8,128)(2,1)} %all-gather.14.cloned.1.call-done), kind=kOutput, calls=%fused_computation.206 | convolution fusion | flops 5771362304 | bytes 15466496 | tf_op jit(solution)/shard_map/dot_general | solution.py:33
  363.9 10.8 multiply_reduce_fusion.4
  386.3 6.6 reshape.268
  399.6 152.8 %while.33 = (s32[]{:T(128)}, f32[4,1024,4,16]{1,3,2,0:T(8,128)}, f32[4,1024,4,16]{1,3,2,0:T(8,128)}, f32[4,1024,4,64]{1,3,2,0:T(8,128)}, bf16[4,1024,4,16]{1,3,2...) while((s32[]{:T(128)}, f32[4,1024,4,16]{1,3,2,0:T(8,128)}, ...), condition=%wide.region_8.9_spmd.clone, body=%wide.region_7.8_spmd.clone.sunk | while | flops 1534201856 | bytes 132695256 | solution.py:252
  399.7 8.2 fusion.207
  408.5 10.8 multiply_convert_fusion.10
  419.3 7.2 fusion.209
  431.9 6.0 fusion.211
  437.8 8.2 fusion.207
  446.6 10.8 multiply_convert_fusion.10
  457.4 7.2 fusion.209
  470.0 6.0 fusion.211
  475.9 8.2 fusion.207
  484.7 10.8 multiply_convert_fusion.10
  495.5 7.2 fusion.209
  508.1 6.0 fusion.211
  514.0 8.2 fusion.207
  522.8 10.8 multiply_convert_fusion.10
  533.6 7.2 fusion.209
  546.2 6.0 fusion.211
  552.5 6.1 fusion.98
  558.8 8.0 fusion.116
  569.5 9.2 convolution_convert_fusion.2
  578.7 9.1 copy.164
  588.7 5.5 add_bitcast_fusion.1
  594.2 15.3 %copy.165 = f32[2,512,16,273]{1,0,3,2:T(2,128)} copy(f32[2,512,16,273]{1,3,2,0:T(8,128)S(1)} %add_bitcast_fusion.1) | data formatting | bytes 35782656 | tf_op jit(solution)/shard_map/reshape | solution.py:267
  609.5 23.4 %reshape.298 = f32[1024,16,273]{0,2,1:T(8,128)} reshape(f32[2,512,16,273]{1,0,3,2:T(2,128)} %copy.165) | data formatting | bytes 35782656 | tf_op jit(solution)/shard_map/reshape | solution.py:267
  632.9 6.0 convolution_convert_fusion.4
  643.0 10.5 fusion.63
  653.5 8.4 copy.144
  662.1 8.1 slice_multiply_fusion.1
  670.2 12.0 %multiply_reduce_fusion.3 = (f32[1024,16,16]{0,2,1:T(8,128)S(1)}, f32[1024,16,16]{0,2,1:T(8,128)S(1)}) fusion(f32[1024,16,16,16]{0,3,2,1:T(8,128)S(1)} %bitcast.295, f32[1024,16,16]{0,2,1:T(8,128)S(1)} %copy-done.8, f32[1024,16,273]{0,2,1:T(8,128)} %reshape.298), kind=kLoop, calls=%fused_computation.64 | loop fusion | flops 20447232 | bytes 37748736 | tf_op jit(solution)/shard_map/transpose(jvp())/reduce_sum | solution.py:20
  682.3 18.4 %convolution_convert_fusion = bf16[1024,5504]{1,0:T(8,128)(2,1)} fusion(bf16[1024,1024]{0,1:T(8,128)(2,1)} %copy-done.27, bf16[1024,2752]{0,1:T(8,128)(2,1)} %get-tuple-element.370, bf16[1024,2752]{0,1:T(8,128)(2,1)} %get-tuple-element.371), kind=kOutput, calls=%fused_computation.67 | convolution fusion | flops 11570905088 | bytes 24641536 | tf_op jit(solution)/shard_map/dot_general | solution.py:39
  701.9 8.0 fusion.71
  713.6 6.5 slice_multiply_fusion
  720.1 12.1 %multiply_reduce_fusion.1 = (f32[1024,16,16]{0,2,1:T(8,128)S(1)}, f32[1024,16,16]{0,2,1:T(8,128)S(1)}) fusion(f32[1024,16,16,16]{0,3,2,1:T(8,128)} %bitcast.296, f32[1024,16,16]{0,2,1:T(8,128)S(1)} %copy-done.11, f32[1024,16,273]{0,2,1:T(8,128)S(1)} %add_bitcast_fusion), kind=kLoop, calls=%fused_computation.62 | loop fusion | flops 20447232 | bytes 37748736 | tf_op jit(solution)/shard_map/transpose(jvp())/reduce_sum | solution.py:20
  737.3 6.1 convolution_convert_fusion.3
  749.1 41.9 %concatenate.35 = bf16[1024,10818]{1,0:T(8,128)(2,1)} concatenate(bf16[1024,1536]{1,0:T(8,128)(2,1)} %convolution_convert_fusion.3, bf16[1024,1024]{1,0:T(8,128)(2,1)} %copy.143, bf16[1024,5504]{1,0:T(8,128)(2,1)} %convolution_convert_fusion, bf16[1024,2752]{1,0:T(8,128)(2,1)} %copy.144, bf16[1024,1]{1,0:T(8,128)(2,1)S(1)} %broadcast_in_dim.128, ...), dimensions={1} | concatenate | bytes 44310528 | tf_op jit(solution)/shard_map/concatenate | solution.py:326
  791.1 218.2 %reduce-scatter.5.cloned.1.call-done = bf16[128,10818]{1,0:T(8,128)(2,1)} async-done(((bf16[1024,10818]{1,0:T(8,128)(2,1)}), bf16[128,10818]{1,0:T(8,128)(2,1)}) %reduce-scatter.5.cloned.1.call-update) | async-done | bytes 2769424 | tf_op jit(solution)/shard_map/reduce_scatter | solution.py:325
  1009.3 11.7 %add_convert_fusion = bf16[1024,1024]{0,1:T(8,128)(2,1)} fusion(f32[1024,1024]{0,1:T(8,128)} %copy-done.12, bf16[1024,2752]{0,1:T(8,128)(2,1)} %get-tuple-element.372, bf16[1024,2752]{0,1:T(8,128)(2,1)} %all-gather.18.cloned.1.call-done), kind=kOutput, calls=%fused_computation.111 | convolution fusion | flops 5773459456 | bytes 17563648 | tf_op jit(solution)/shard_map/dot_general | solution.py:33
  1025.0 6.6 fusion.68
  1031.6 5.4 copy.148
  1037.0 55.2 %all-reduce.2.cloned.1.call-done = bf16[128,10818]{1,0:T(8,128)(2,1)} async-done(((bf16[128,10818]{1,0:T(8,128)(2,1)}), bf16[128,10818]{1,0:T(8,128)(2,1)}) %all-reduce.2.cloned.1.call-update) | async-done | bytes 2769424 | tf_op jit(solution)/shard_map/psum | solution.py:341
  (289 shorter events, 168.0 us)
Async XLA Ops:
  7.2 17.7 %copy-start.35 = (bf16[128,256]{1,0:T(8,128)(2,1)S(1)}, bf16[128,256]{1,0:T(8,128)(2,1)}, u32[]{:S(2)}) copy-start(bf16[128,256]{1,0:T(8,128)(2,1)} %param.19) | copy-start | bytes 196612
  7.2 47.4 %all-gather.10.cloned.1.call-start = ((), (), s32[]{:S(2)}) async-start(), calls=%async_computation.2 | async-start | bytes 2359296 | tf_op jit(solution)/shard_map/all_gather | solution.py:158
  7.9 190.4 %all-gather.20.cloned.1.call-start = ((), (), s32[]{:S(2)}) async-start(), calls=%async_computation.10 | async-start | bytes 5806080 | tf_op jit(solution)/shard_map/all_gather | solution.py:180
  10.8 216.3 %copy-start.5 = (bf16[1024,1024]{0,1:T(8,128)(2,1)}, bf16[1024,1024]{0,1:T(8,128)(2,1)S(1)}, u32[]{:S(2)}) copy-start(bf16[1024,1024]{0,1:T(8,128)(2,1)S(1)} %copy.120) | copy-start | bytes 6291460
  24.3 67.3 %copy-start.40 = (f32[8,1,128]{2,1,0:T(1,128)}, f32[8,1,128]{2,1,0:T(1,128)S(1)}, u32[]{:S(2)}) copy-start(f32[8,1,128]{2,1,0:T(1,128)S(1)} %convert_element_type.208) | copy-start | bytes 12292
  24.4 116.6 %copy-start.44 = (bf16[273]{0:T(512)(128)(2,1)}, bf16[273]{0:T(512)(128)(2,1)S(1)}, u32[]{:S(2)}) copy-start(bf16[273]{0:T(512)(128)(2,1)S(1)} %pad.12.clone) | copy-start | bytes 1642
  24.9 66.8 %copy-start.42 = (f32[1024]{0:T(1024)}, f32[1024]{0:T(1024)S(1)}, u32[]{:S(2)}) copy-start(f32[1024]{0:T(1024)S(1)} %add_rsqrt_fusion.1) | copy-start | bytes 12292
  43.0 5.9 copy-start.10
  43.2 15.8 %copy-start.31 = (bf16[1024,16,16]{0,2,1:T(8,128)(2,1)}, bf16[1024,16,16]{0,2,1:T(8,128)(2,1)S(1)}, u32[]{:S(2)}) copy-start(bf16[1024,16,16]{0,2,1:T(8,128)(2,1)S(1)} %multiply_convert_fusion.8) | copy-start | bytes 1572868
  54.6 4.4 copy-start.17
  58.9 4.4 copy-start.15
  63.3 4.9 copy-start.54
  63.3 8.8 copy-start.53
  63.3 10.7 copy-start.36
  65.7 161.5 %all-gather.12.cloned.1.call-start = ((), (), s32[]{:S(2)}) async-start(), calls=%async_computation.3 | async-start | bytes 2359296 | tf_op jit(solution)/shard_map/all_gather | solution.py:14
  66.4 167.8 %all-gather.14.cloned.1.call-start = ((), (), s32[]{:S(2)}) async-start(), calls=%async_computation.4 | async-start | bytes 6340608 | tf_op jit(solution)/shard_map/all_gather | solution.py:213
  67.0 206.3 %all-gather.16.cloned.1.call-start = ((), (), s32[]{:S(2)}) async-start(), calls=%async_computation.5 | async-start | bytes 6340608 | tf_op jit(solution)/shard_map/all_gather | solution.py:214
  67.6 265.1 %all-gather.18.cloned.1.call-start = ((), (), s32[]{:S(2)}) async-start(), calls=%async_computation.6 | async-start | bytes 6340608 | tf_op jit(solution)/shard_map/all_gather | solution.py:14
  68.1 632.5 %reduce-scatter.3.cloned.1.call-start = ((), (), s32[]{:S(2)}) async-start(), calls=%async_computation.7 | async-start | bytes 7188480 | tf_op jit(solution)/shard_map/reduce_scatter | solution.py:276
  73.3 125.0 %copy-start.51 = (pred[1,8]{1,0:T(4,128)(4,1)}, pred[1,8]{1,0:T(4,128)(4,1)S(1)}, u32[]{:S(2)}) copy-start(pred[1,8]{1,0:T(4,128)(4,1)S(1)} %get-tuple-element.366) | copy-start | bytes 28
  114.8 12.7 %copy-start.56 = (bf16[128]{0:T(256)(128)(2,1)S(1)}, bf16[128]{0:T(256)(128)(2,1)}, u32[]{:S(2)}) copy-start(bf16[128]{0:T(256)(128)(2,1)} %param.26) | copy-start | bytes 772
  153.4 45.0 %copy-start.47 = (pred[1,8]{1,0:T(4,128)(4,1)}, pred[1,8]{1,0:T(4,128)(4,1)S(1)}, u32[]{:S(2)}) copy-start(pred[1,8]{1,0:T(4,128)(4,1)S(1)} %get-tuple-element.384) | copy-start | bytes 28
  153.4 45.0 %copy-start.49 = (pred[1,8]{1,0:T(4,128)(4,1)}, pred[1,8]{1,0:T(4,128)(4,1)S(1)}, u32[]{:S(2)}) copy-start(pred[1,8]{1,0:T(4,128)(4,1)S(1)} %get-tuple-element.385) | copy-start | bytes 28
  209.5 6.7 copy-start.14
  216.2 6.2 slice-start.4
  216.2 6.2 slice-start.5
  247.0 85.6 %copy-start.25 = (bf16[1024,1024]{1,0:T(8,128)(2,1)S(1)}, bf16[1024,1024]{1,0:T(8,128)(2,1)}, u32[]{:S(2)}) copy-start(bf16[1024,1024]{1,0:T(8,128)(2,1)} %param.29) | copy-start | bytes 6291460
  352.6 11.3 %copy-start.13 = (f32[1024,1024]{0,1:T(8,128)S(1)}, f32[1024,1024]{0,1:T(8,128)}, u32[]{:S(2)}) copy-start(f32[1024,1024]{0,1:T(8,128)} %copy-done.12) | copy-start | bytes 12582916
  352.6 11.3 %copy-start.57 = (bf16[1024,2752]{0,1:T(8,128)(2,1)S(1)}, bf16[1024,2752]{0,1:T(8,128)(2,1)}, u32[]{:S(2)}) copy-start(bf16[1024,2752]{0,1:T(8,128)(2,1)} %all-gather.16.cloned.1.call-done) | copy-start | bytes 16908292
  363.9 10.8 copy-start.1
  376.3 4.4 copy-start.21
  377.3 8.1 copy-start.4
  399.6 152.8 %copy-start.30 = (f32[2,16,1,512]{3,2,1,0:T(1,128)S(1)}, f32[2,16,1,512]{3,2,1,0:T(1,128)}, u32[]{:S(2)}) copy-start(f32[2,16,1,512]{3,2,1,0:T(1,128)} %copy-done.29) | copy-start | bytes 196612
  399.6 152.8 %copy-start.33 = (f32[2,512,16]{1,0,2:T(2,128)S(1)}, f32[2,512,16]{1,0,2:T(2,128)}, u32[]{:S(2)}) copy-start(f32[2,512,16]{1,0,2:T(2,128)} %reshape.269) | copy-start | bytes 196612
  399.6 152.8 %copy-start.34 = (f32[2,512,16]{1,0,2:T(2,128)S(1)}, f32[2,512,16]{1,0,2:T(2,128)}, u32[]{:S(2)}) copy-start(f32[2,512,16]{1,0,2:T(2,128)} %neg.17) | copy-start | bytes 196612
  408.5 23.3 %slice-start = ((s8[16777216]{0:T(1024)(128)(4,1)}), s8[4194304]{0:T(1024)(128)(4,1)S(1)}, s32[]{:S(2)}) async-start(s8[16777216]{0:T(1024)(128)(4,1)} %bitcast.291), calls=%async_computation.11 | async-start | bytes 8388608 | tf_op jit(solution)/shard_map/while
  408.5 23.3 %slice-start.1 = ((s8[16777216]{0:T(1024)(128)(4,1)}), s8[4194304]{0:T(1024)(128)(4,1)S(1)}, s32[]{:S(2)}) async-start(s8[16777216]{0:T(1024)(128)(4,1)} %bitcast.291), calls=%async_computation.12 | async-start | bytes 8388608 | tf_op jit(solution)/shard_map/while
  408.5 23.3 %slice-start.2 = ((s8[16777216]{0:T(1024)(128)(4,1)}), s8[4194304]{0:T(1024)(128)(4,1)S(1)}, s32[]{:S(2)}) async-start(s8[16777216]{0:T(1024)(128)(4,1)} %bitcast.291), calls=%async_computation.13 | async-start | bytes 8388608 | tf_op jit(solution)/shard_map/while
  419.3 12.5 %slice-start.3 = ((s8[16777216]{0:T(1024)(128)(4,1)}), s8[4194304]{0:T(1024)(128)(4,1)S(1)}, s32[]{:S(2)}) async-start(s8[16777216]{0:T(1024)(128)(4,1)} %bitcast.291), calls=%async_computation.14 | async-start | bytes 8388608 | tf_op jit(solution)/shard_map/while
  446.6 23.3 %slice-start = ((s8[16777216]{0:T(1024)(128)(4,1)}), s8[4194304]{0:T(1024)(128)(4,1)S(1)}, s32[]{:S(2)}) async-start(s8[16777216]{0:T(1024)(128)(4,1)} %bitcast.291), calls=%async_computation.11 | async-start | bytes 8388608 | tf_op jit(solution)/shard_map/while
  446.6 23.3 %slice-start.1 = ((s8[16777216]{0:T(1024)(128)(4,1)}), s8[4194304]{0:T(1024)(128)(4,1)S(1)}, s32[]{:S(2)}) async-start(s8[16777216]{0:T(1024)(128)(4,1)} %bitcast.291), calls=%async_computation.12 | async-start | bytes 8388608 | tf_op jit(solution)/shard_map/while
  446.6 23.3 %slice-start.2 = ((s8[16777216]{0:T(1024)(128)(4,1)}), s8[4194304]{0:T(1024)(128)(4,1)S(1)}, s32[]{:S(2)}) async-start(s8[16777216]{0:T(1024)(128)(4,1)} %bitcast.291), calls=%async_computation.13 | async-start | bytes 8388608 | tf_op jit(solution)/shard_map/while
  457.4 12.5 %slice-start.3 = ((s8[16777216]{0:T(1024)(128)(4,1)}), s8[4194304]{0:T(1024)(128)(4,1)S(1)}, s32[]{:S(2)}) async-start(s8[16777216]{0:T(1024)(128)(4,1)} %bitcast.291), calls=%async_computation.14 | async-start | bytes 8388608 | tf_op jit(solution)/shard_map/while
  484.7 23.3 %slice-start = ((s8[16777216]{0:T(1024)(128)(4,1)}), s8[4194304]{0:T(1024)(128)(4,1)S(1)}, s32[]{:S(2)}) async-start(s8[16777216]{0:T(1024)(128)(4,1)} %bitcast.291), calls=%async_computation.11 | async-start | bytes 8388608 | tf_op jit(solution)/shard_map/while
  484.7 23.3 %slice-start.1 = ((s8[16777216]{0:T(1024)(128)(4,1)}), s8[4194304]{0:T(1024)(128)(4,1)S(1)}, s32[]{:S(2)}) async-start(s8[16777216]{0:T(1024)(128)(4,1)} %bitcast.291), calls=%async_computation.12 | async-start | bytes 8388608 | tf_op jit(solution)/shard_map/while
  484.7 23.3 %slice-start.2 = ((s8[16777216]{0:T(1024)(128)(4,1)}), s8[4194304]{0:T(1024)(128)(4,1)S(1)}, s32[]{:S(2)}) async-start(s8[16777216]{0:T(1024)(128)(4,1)} %bitcast.291), calls=%async_computation.13 | async-start | bytes 8388608 | tf_op jit(solution)/shard_map/while
  495.5 12.5 %slice-start.3 = ((s8[16777216]{0:T(1024)(128)(4,1)}), s8[4194304]{0:T(1024)(128)(4,1)S(1)}, s32[]{:S(2)}) async-start(s8[16777216]{0:T(1024)(128)(4,1)} %bitcast.291), calls=%async_computation.14 | async-start | bytes 8388608 | tf_op jit(solution)/shard_map/while
  522.8 23.3 %slice-start = ((s8[16777216]{0:T(1024)(128)(4,1)}), s8[4194304]{0:T(1024)(128)(4,1)S(1)}, s32[]{:S(2)}) async-start(s8[16777216]{0:T(1024)(128)(4,1)} %bitcast.291), calls=%async_computation.11 | async-start | bytes 8388608 | tf_op jit(solution)/shard_map/while
  522.8 23.3 %slice-start.1 = ((s8[16777216]{0:T(1024)(128)(4,1)}), s8[4194304]{0:T(1024)(128)(4,1)S(1)}, s32[]{:S(2)}) async-start(s8[16777216]{0:T(1024)(128)(4,1)} %bitcast.291), calls=%async_computation.12 | async-start | bytes 8388608 | tf_op jit(solution)/shard_map/while
  522.8 23.3 %slice-start.2 = ((s8[16777216]{0:T(1024)(128)(4,1)}), s8[4194304]{0:T(1024)(128)(4,1)S(1)}, s32[]{:S(2)}) async-start(s8[16777216]{0:T(1024)(128)(4,1)} %bitcast.291), calls=%async_computation.13 | async-start | bytes 8388608 | tf_op jit(solution)/shard_map/while
  533.6 12.5 %slice-start.3 = ((s8[16777216]{0:T(1024)(128)(4,1)}), s8[4194304]{0:T(1024)(128)(4,1)S(1)}, s32[]{:S(2)}) async-start(s8[16777216]{0:T(1024)(128)(4,1)} %bitcast.291), calls=%async_computation.14 | async-start | bytes 8388608 | tf_op jit(solution)/shard_map/while
  558.8 8.0 copy-start.37
  587.8 421.5 %reduce-scatter.5.cloned.1.call-start = ((), (), s32[]{:S(2)}) async-start(), calls=%async_computation.8 | async-start | bytes 25067520 | tf_op jit(solution)/shard_map/reduce_scatter | solution.py:325
  609.5 23.4 %copy-start.22 = (bf16[1024,1024]{0,1:T(8,128)(2,1)S(1)}, bf16[1024,1024]{0,1:T(8,128)(2,1)}, u32[]{:S(2)}) copy-start(bf16[1024,1024]{0,1:T(8,128)(2,1)} %fusion.75) | copy-start | bytes 6291460
  653.5 8.4 copy-start.46
  662.1 8.1 copy-start.8
  682.3 19.6 %copy-start.32 = (bf16[1024,16,16]{0,2,1:T(8,128)(2,1)S(1)}, bf16[1024,16,16]{0,2,1:T(8,128)(2,1)}, u32[]{:S(2)}) copy-start(bf16[1024,16,16]{0,2,1:T(8,128)(2,1)} %copy-done.31) | copy-start | bytes 1572868
  682.3 19.6 %copy-start.45 = (bf16[273]{0:T(512)(128)(2,1)S(1)}, bf16[273]{0:T(512)(128)(2,1)}, u32[]{:S(2)}) copy-start(bf16[273]{0:T(512)(128)(2,1)} %copy-done.44) | copy-start | bytes 1642
  701.9 8.7 copy-start.16
  713.6 6.5 copy-start.11
  720.1 12.1 %copy-start.28 = (f32[4,1024,4,16]{1,3,2,0:T(8,128)S(1)}, f32[4,1024,4,16]{1,3,2,0:T(8,128)}, u32[]{:S(2)}) copy-start(f32[4,1024,4,16]{1,3,2,0:T(8,128)} %get-tuple-element.230) | copy-start | bytes 3145732
  737.3 6.1 copy-start.58
  791.0 301.1 %all-reduce.2.cloned.1.call-start = ((), (), s32[]{:S(2)}) async-start(), calls=%async_computation.9 | async-start | bytes 5570560 | tf_op jit(solution)/shard_map/psum | solution.py:341
  1096.1 8.8 copy-start.9
  (24 other events, 49.9 us)
Sparse Core Ops, SparseCore 0:
  9.6 36.0 all-gather.9
  65.8 57.8 all-gather.19
  125.3 27.8 all-gather.11
  154.7 59.1 all-gather.13
  215.3 57.9 all-gather.15
  274.7 57.9 all-gather.17
  588.0 69.0 reduce-scatter.2
  791.2 218.1 reduce-scatter.4
  1012.5 79.6 all-reduce.1
where the time goes:
time: 1130 us; the launch traced here: 1110 us
  matrix products  391 us (35%)
  waiting for transfers between devices  351 us (31%)
  local copies, waits for them, and re-layouts  204 us (18%)
  other arithmetic  90.3 us (8%)
  blocking collectives  57.8 us (5%)
  between operations  19.1 us (2%)
    reduce_scatter x1, waiting for transfers between devices, local(): lax.psum_scatter(jnp.concatenate([contract_first(pick(hidden_one), grad_q...  218 us
    dot_general x8, matrix products, kernel_of(): jnp.einsum('thf,uhf->htu', queries, key_heads, preferred_element_type=jnp...  57.4 us
    psum x1, waiting for transfers between devices, local(): own_grads = lax.psum(group_share, 'rep').astype(jnp.float32)  55.2 us
    all_gather x2, waiting for transfers between devices, on_whole(): whole = lax.all_gather(value, axis, axis=dim, tiled=True)  48.3 us
    dot_general x7, matrix products, contract_last(): lax.dot_general(left, right, (((1,), (1,)), ((), ())), preferred_element_...  44.6 us
    dot_general x4, matrix products, local_backward(): jnp.einsum('the,uhe->htu', grad_num, value_heads, preferred_element_type=...  43.1 us
    concatenate x1, local copies, waits for them, and re-layouts, local(): jnp.concatenate([contract_first(pick(hidden_one), grad_qkv), contract_fir...  41.9 us
    dot_general x4, matrix products, contract_first(): lax.dot_general(left, right, (((0,), (0,)), ((), ())), preferred_element_...  40.9 us
  transfers between devices with their start and end apart: 9, of which 4 were waited for; matrix products, arithmetic and copies ran while one was open for 28% of the time, Pallas kernels for 0%

commit v1 on v0

--- a/solution.py
+++ b/solution.py
@@ -4,6 +4,7 @@
 import jax.numpy as jnp
 from jax import lax
 from jax.sharding import PartitionSpec as P
+from jax.lax import all_gather
 
 HEADS = 16
 CONT_PER = 4
@@ -338,7 +339,7 @@
         scatter_dimension=0,
         tiled=True,
     )
-    own_grads = lax.psum(group_share, "rep").astype(jnp.float32)
+    own_grads = jnp.sum(all_gather(group_share, "rep"), axis=0).astype(jnp.float32)
     edge_two = qk_width + qk_width
     edge_three = edge_two + value_width
     edge_four = edge_three + value_width

time: 1130 us -> 1160 us (1.027)
  waiting for transfers between devices: 351 us -> 379 us
    all_gather x0 -> x1, waiting for transfers between devices: none -> 83.1 us  [local(): all_gather(group_share, 'rep')]
    psum x1 -> x0, waiting for transfers between devices: 55.2 us -> none  [local(): own_grads = lax.psum(group_share, 'rep').astype(jnp.float32)]
  transfers between devices with their start and end apart: 9 -> 9, of which waited for: 4 -> 4; matrix products, arithmetic and copies ran while one was open for 28% -> 27% of each run, Pallas kernels for 0% -> 0%
where the time goes in v1:
time: 1160 us; the launch traced here: 1150 us
  matrix products  391 us (34%)
  waiting for transfers between devices  379 us (33%)
  local copies, waits for them, and re-layouts  202 us (17%)
  other arithmetic  98.7 us (9%)
  blocking collectives  57.8 us (5%)
  between operations  19.1 us (2%)
    reduce_scatter x1, waiting for transfers between devices, local(): lax.psum_scatter(jnp.concatenate([contract_first(pick(hidden_one), grad_q...  218 us
    all_gather x1, waiting for transfers between devices, local(): all_gather(group_share, 'rep')  83.1 us
    dot_general x8, matrix products, kernel_of(): jnp.einsum('thf,uhf->htu', queries, key_heads, preferred_element_type=jnp...  57.4 us
    all_gather x2, waiting for transfers between devices, on_whole(): whole = lax.all_gather(value, axis, axis=dim, tiled=True)  48.3 us
    dot_general x7, matrix products, contract_last(): lax.dot_general(left, right, (((1,), (1,)), ((), ())), preferred_element_...  44.6 us
    dot_general x4, matrix products, local_backward(): jnp.einsum('the,uhe->htu', grad_num, value_heads, preferred_element_type=...  43.1 us
    concatenate x1, local copies, waits for them, and re-layouts, local(): jnp.concatenate([contract_first(pick(hidden_one), grad_qkv), contract_fir...  41.9 us
    dot_general x4, matrix products, contract_first(): lax.dot_general(left, right, (((0,), (0,)), ((), ())), preferred_element_...  40.9 us
  transfers between devices with their start and end apart: 9, of which 4 were waited for; matrix products, arithmetic and copies ran while one was open for 27% of the time, Pallas kernels for 0%

profile of v1, /device:TPU:0, one launch (start us, length us, event | category | flops | bytes accessed | tf_op | source)
XLA Modules:
  0.0 1149.1 jit_solution(10273940848879646815)
XLA Ops:
  10.9 13.5 %all-gather.1 = bf16[8,1,128]{2,1,0:T(2,128)(2,1)S(1)} all-gather(bf16[1,1,128]{2,1,0:T(2,128)(2,1)S(1)} %bitcast.341), channel_id=1, replica_groups=mesh['rep'=4,'shard'=8] {'shard'}, dimensions={0}, use_global_device_ids=true | all-gather | bytes 2304 | tf_op jit(solution)/shard_map/all_gather | solution.py:160
  24.9 17.3 %all_gather.46 = bf16[1024,256]{1,0:T(8,128)(2,1)S(1)} all-gather(bf16[128,256]{1,0:T(8,128)(2,1)S(1)} %copy-done.35), channel_id=1, replica_groups=mesh['rep'=4,'shard'=8] {'shard'}, dimensions={0}, use_global_device_ids=true | all-gather | bytes 589824 | tf_op jit(solution)/shard_map/all_gather | solution.py:158
  43.2 5.8 multiply_convert_fusion.2
  48.9 5.5 fusion.107
  74.0 17.6 %all_gather.45 = bf16[1024,256]{1,0:T(8,128)(2,1)S(1)} all-gather(bf16[128,256]{1,0:T(8,128)(2,1)S(1)} %copy-done.36), channel_id=1, replica_groups=mesh['rep'=4,'shard'=8] {'shard'}, dimensions={0}, use_global_device_ids=true | all-gather | bytes 589824 | tf_op jit(solution)/shard_map/all_gather | solution.py:157
  94.5 5.7 multiply_convert_fusion.1
  100.2 14.6 %div.136 = bf16[2,512,16,256]{1,0,3,2:T(2,128)(2,1)} reshape(bf16[1024,16,16,16]{0,3,2,1:T(8,128)(2,1)} %multiply_convert_fusion.1) | data formatting | bytes 16777216 | tf_op jit(solution)/shard_map/div | solution.py:27
  114.8 8.6 copy.161
  127.5 9.4 all-gather.3
  140.9 11.8 %pad_maximum_fusion.1 = bf16[2,512,16,273]{1,3,2,0:T(8,128)(2,1)} fusion(bf16[2,512,16,256]{1,3,2,0:T(8,128)(2,1)} %copy.161, bf16[2,512,16,16]{1,3,2,0:T(8,128)(2,1)} %copy.160, bf16[273]{0:T(512)(128)(2,1)S(1)} %pad.12.clone), kind=kLoop, calls=%fused_computation.76 | loop fusion | flops 26836992 | bytes 17859106 | tf_op jit(solution)/shard_map/concatenate | solution.py:23
  156.0 41.7 %while.32 = (s32[]{:T(128)}, f32[4,1024,4,64]{1,3,2,0:T(8,128)}, f32[4,1024,4]{1,2,0:T(4,128)S(1)}, bf16[4,1024,4,64]{1,3,2,0:T(8,128)(2,1)}, bf16[4,1024,4,16]{...) while((s32[]{:T(128)}, f32[4,1024,4,64]{1,3,2,0:T(8,128)}, ...), condition=%wide.region_3.4_spmd.clone, body=%wide.region_1.3_spmd.clone.sunk | while | flops 707784704 | bytes 20764768 | solution.py:200
  156.6 6.2 fusion.196
  167.0 6.2 fusion.196
  177.4 6.2 fusion.196
  187.8 6.2 fusion.196
  209.5 6.7 fusion.127
  235.5 11.5 fusion.129
  247.0 26.2 %all-gather.18.cloned.1.call-done = bf16[1024,2752]{0,1:T(8,128)(2,1)} async-done(((bf16[128,2752]{0,1:T(8,128)(2,1)}), bf16[1024,2752]{0,1:T(8,128)(2,1)}) %all-gather.18.cloned.1.call-update) | async-done | bytes 5636112 | tf_op jit(solution)/shard_map/all_gather | solution.py:215
  273.2 11.1 fusion.130
  284.3 48.3 %all-gather.20.cloned.1.call-done = bf16[1024,2752]{0,1:T(8,128)(2,1)} async-done(((bf16[128,2752]{0,1:T(8,128)(2,1)}), bf16[1024,2752]{0,1:T(8,128)(2,1)}) %all-gather.20.cloned.1.call-update) | async-done | bytes 5636112 | tf_op jit(solution)/shard_map/all_gather | solution.py:15
  332.6 20.0 %multiply_convert_fusion.3 = (bf16[1024,2752]{0,1:T(8,128)(2,1)}, bf16[1024,2752]{0,1:T(8,128)(2,1)}, bf16[1024,2752]{0,1:T(8,128)(2,1)}) fusion(f32[1024,2752]{0,1:T(8,128)} %fusion.129, f32[1024,2752]{0,1:T(8,128)} %fusion.130, bf16[1024,1024]{1,0:T(8,128)(2,1)S(1)} %copy-done.25, bf16[1024,2752]{0,1:T(8,128)(2,1)} %all-gather.20.cloned.1.call-done), kind=kOutput, calls=%fused_computation.71 | convolution fusion | flops 5816451072 | bytes 47185920 | tf_op jit(solution)/shard_map/dot_general | solution.py:227
  352.6 11.3 fusion.128
  363.9 10.8 multiply_reduce_fusion.4
  386.3 6.6 reshape.268
  399.6 152.8 %while.33 = (s32[]{:T(128)}, f32[4,1024,4,16]{1,3,2,0:T(8,128)}, f32[4,1024,4,16]{1,3,2,0:T(8,128)}, f32[4,1024,4,64]{1,3,2,0:T(8,128)}, bf16[4,1024,4,16]{1,3,2...) while((s32[]{:T(128)}, f32[4,1024,4,16]{1,3,2,0:T(8,128)}, ...), condition=%wide.region_8.9_spmd.clone, body=%wide.region_7.8_spmd.clone.sunk | while | flops 1534201856 | bytes 132695256 | solution.py:253
  399.7 8.2 fusion.207
  408.5 10.8 multiply_convert_fusion.10
  419.3 7.2 fusion.209
  431.9 6.0 fusion.211
  437.8 8.2 fusion.207
  446.6 10.8 multiply_convert_fusion.10
  457.4 7.2 fusion.209
  470.0 6.0 fusion.211
  475.9 8.2 fusion.207
  484.7 10.8 multiply_convert_fusion.10
  495.5 7.2 fusion.209
  508.1 6.0 fusion.211
  514.0 8.2 fusion.207
  522.8 10.8 multiply_convert_fusion.10
  533.6 7.2 fusion.209
  546.2 6.0 fusion.211
  552.5 6.1 fusion.98
  558.8 8.0 fusion.116
  569.5 9.2 convolution_convert_fusion.2
  578.7 9.1 copy.200
  588.7 5.5 add_bitcast_fusion.1
  594.2 15.3 %copy.201 = f32[2,512,16,273]{1,0,3,2:T(2,128)} copy(f32[2,512,16,273]{1,3,2,0:T(8,128)S(1)} %add_bitcast_fusion.1) | data formatting | bytes 35782656 | tf_op jit(solution)/shard_map/reshape | solution.py:268
  609.5 23.4 %reshape.299 = f32[1024,16,273]{0,2,1:T(8,128)} reshape(f32[2,512,16,273]{1,0,3,2:T(2,128)} %copy.201) | data formatting | bytes 35782656 | tf_op jit(solution)/shard_map/reshape | solution.py:268
  632.9 6.0 convolution_convert_fusion.4
  643.0 10.5 fusion.63
  653.5 8.4 copy.180
  662.1 8.1 slice_multiply_fusion.1
  670.2 12.0 %multiply_reduce_fusion.3 = (f32[1024,16,16]{0,2,1:T(8,128)S(1)}, f32[1024,16,16]{0,2,1:T(8,128)S(1)}) fusion(f32[1024,16,16,16]{0,3,2,1:T(8,128)S(1)} %bitcast.296, f32[1024,16,16]{0,2,1:T(8,128)S(1)} %copy-done.8, f32[1024,16,273]{0,2,1:T(8,128)} %reshape.299), kind=kLoop, calls=%fused_computation.64 | loop fusion | flops 20447232 | bytes 37748736 | tf_op jit(solution)/shard_map/transpose(jvp())/reduce_sum | solution.py:21
  682.3 18.4 %convolution_convert_fusion = bf16[1024,5504]{1,0:T(8,128)(2,1)} fusion(bf16[1024,1024]{0,1:T(8,128)(2,1)} %copy-done.27, bf16[1024,2752]{0,1:T(8,128)(2,1)} %get-tuple-element.381, bf16[1024,2752]{0,1:T(8,128)(2,1)} %get-tuple-element.382), kind=kOutput, calls=%fused_computation.67 | convolution fusion | flops 11570905088 | bytes 24641536 | tf_op jit(solution)/shard_map/dot_general | solution.py:40
  701.9 8.0 fusion.71
  713.6 6.5 slice_multiply_fusion
  720.1 12.1 %multiply_reduce_fusion.1 = (f32[1024,16,16]{0,2,1:T(8,128)S(1)}, f32[1024,16,16]{0,2,1:T(8,128)S(1)}) fusion(f32[1024,16,16,16]{0,3,2,1:T(8,128)} %bitcast.297, f32[1024,16,16]{0,2,1:T(8,128)S(1)} %copy-done.10, f32[1024,16,273]{0,2,1:T(8,128)S(1)} %add_bitcast_fusion), kind=kLoop, calls=%fused_computation.62 | loop fusion | flops 20447232 | bytes 37748736 | tf_op jit(solution)/shard_map/transpose(jvp())/reduce_sum | solution.py:21
  737.3 6.1 convolution_convert_fusion.3
  749.1 41.9 %concatenate.35 = bf16[1024,10818]{1,0:T(8,128)(2,1)} concatenate(bf16[1024,1536]{1,0:T(8,128)(2,1)} %convolution_convert_fusion.3, bf16[1024,1024]{1,0:T(8,128)(2,1)} %copy.179, bf16[1024,5504]{1,0:T(8,128)(2,1)} %convolution_convert_fusion, bf16[1024,2752]{1,0:T(8,128)(2,1)} %copy.180, bf16[1024,1]{1,0:T(8,128)(2,1)S(1)} %broadcast_in_dim.128, ...), dimensions={1} | concatenate | bytes 44310528 | tf_op jit(solution)/shard_map/concatenate | solution.py:327
  791.1 218.2 %reduce-scatter.5.cloned.1.call-done = bf16[128,10818]{1,0:T(8,128)(2,1)} async-done(((bf16[1024,10818]{1,0:T(8,128)(2,1)}), bf16[128,10818]{1,0:T(8,128)(2,1)}) %reduce-scatter.5.cloned.1.call-update) | async-done | bytes 2769424 | tf_op jit(solution)/shard_map/reduce_scatter | solution.py:326
  1009.3 11.7 %add_convert_fusion = bf16[1024,1024]{0,1:T(8,128)(2,1)} fusion(f32[1024,1024]{0,1:T(8,128)} %copy-done.11, bf16[1024,2752]{0,1:T(8,128)(2,1)} %get-tuple-element.383, bf16[1024,2752]{0,1:T(8,128)(2,1)} %all-gather.20.cloned.1.call-done), kind=kOutput, calls=%fused_computation.111 | convolution fusion | flops 5773459456 | bytes 17563648 | tf_op jit(solution)/shard_map/dot_general | solution.py:34
  1025.2 6.4 fusion.68
  1037.0 83.1 %all-gather.22.cloned.1.call-done = bf16[512,10818]{1,0:T(8,128)(2,1)} async-done(((bf16[128,10818]{1,0:T(8,128)(2,1)}), bf16[512,10818]{1,0:T(8,128)(2,1)}) %all-gather.22.cloned.1.call-update) | async-done | bytes 11077648 | tf_op jit(solution)/shard_map/all_gather | solution.py:342
  1120.1 6.1 reduce_sum.150
  (290 shorter events, 173.9 us)
Async XLA Ops:
  7.2 17.7 %copy-start.35 = (bf16[128,256]{1,0:T(8,128)(2,1)S(1)}, bf16[128,256]{1,0:T(8,128)(2,1)}, u32[]{:S(2)}) copy-start(bf16[128,256]{1,0:T(8,128)(2,1)} %param.19) | copy-start | bytes 196612
  7.2 47.4 %all-gather.12.cloned.1.call-start = ((), (), s32[]{:S(2)}) async-start(), calls=%async_computation.2 | async-start | bytes 2359296 | tf_op jit(solution)/shard_map/all_gather | solution.py:159
  7.9 190.4 %all-gather.24.cloned.1.call-start = ((), (), s32[]{:S(2)}) async-start(), calls=%async_computation.10 | async-start | bytes 5806080 | tf_op jit(solution)/shard_map/all_gather | solution.py:181
  10.8 216.3 %copy-start.5 = (bf16[1024,1024]{0,1:T(8,128)(2,1)}, bf16[1024,1024]{0,1:T(8,128)(2,1)S(1)}, u32[]{:S(2)}) copy-start(bf16[1024,1024]{0,1:T(8,128)(2,1)S(1)} %copy.156) | copy-start | bytes 6291460
  24.3 67.3 %copy-start.40 = (f32[8,1,128]{2,1,0:T(1,128)}, f32[8,1,128]{2,1,0:T(1,128)S(1)}, u32[]{:S(2)}) copy-start(f32[8,1,128]{2,1,0:T(1,128)S(1)} %convert_element_type.210) | copy-start | bytes 12292
  24.4 116.6 %copy-start.44 = (bf16[273]{0:T(512)(128)(2,1)}, bf16[273]{0:T(512)(128)(2,1)S(1)}, u32[]{:S(2)}) copy-start(bf16[273]{0:T(512)(128)(2,1)S(1)} %pad.12.clone) | copy-start | bytes 1642
  24.9 66.8 %copy-start.42 = (f32[1024]{0:T(1024)}, f32[1024]{0:T(1024)S(1)}, u32[]{:S(2)}) copy-start(f32[1024]{0:T(1024)S(1)} %add_rsqrt_fusion.1) | copy-start | bytes 12292
  43.0 5.9 copy-start.9
  43.2 15.8 %copy-start.31 = (bf16[1024,16,16]{0,2,1:T(8,128)(2,1)}, bf16[1024,16,16]{0,2,1:T(8,128)(2,1)S(1)}, u32[]{:S(2)}) copy-start(bf16[1024,16,16]{0,2,1:T(8,128)(2,1)S(1)} %multiply_convert_fusion.8) | copy-start | bytes 1572868
  54.6 4.4 copy-start.16
  58.9 4.4 copy-start.14
  63.3 4.9 copy-start.54
  63.3 8.8 copy-start.53
  63.3 10.7 copy-start.36
  65.7 161.5 %all-gather.14.cloned.1.call-start = ((), (), s32[]{:S(2)}) async-start(), calls=%async_computation.3 | async-start | bytes 2359296 | tf_op jit(solution)/shard_map/all_gather | solution.py:15
  66.4 167.8 %all-gather.16.cloned.1.call-start = ((), (), s32[]{:S(2)}) async-start(), calls=%async_computation.4 | async-start | bytes 6340608 | tf_op jit(solution)/shard_map/all_gather | solution.py:214
  67.0 206.3 %all-gather.18.cloned.1.call-start = ((), (), s32[]{:S(2)}) async-start(), calls=%async_computation.5 | async-start | bytes 6340608 | tf_op jit(solution)/shard_map/all_gather | solution.py:215
  67.6 265.1 %all-gather.20.cloned.1.call-start = ((), (), s32[]{:S(2)}) async-start(), calls=%async_computation.6 | async-start | bytes 6340608 | tf_op jit(solution)/shard_map/all_gather | solution.py:15
  68.1 632.5 %reduce-scatter.3.cloned.1.call-start = ((), (), s32[]{:S(2)}) async-start(), calls=%async_computation.7 | async-start | bytes 7188480 | tf_op jit(solution)/shard_map/reduce_scatter | solution.py:277
  73.3 125.0 %copy-start.51 = (pred[1,8]{1,0:T(4,128)(4,1)}, pred[1,8]{1,0:T(4,128)(4,1)S(1)}, u32[]{:S(2)}) copy-start(pred[1,8]{1,0:T(4,128)(4,1)S(1)} %get-tuple-element.377) | copy-start | bytes 28
  114.8 12.7 %copy-start.56 = (bf16[128]{0:T(256)(128)(2,1)S(1)}, bf16[128]{0:T(256)(128)(2,1)}, u32[]{:S(2)}) copy-start(bf16[128]{0:T(256)(128)(2,1)} %param.26) | copy-start | bytes 772
  153.4 45.0 %copy-start.47 = (pred[1,8]{1,0:T(4,128)(4,1)}, pred[1,8]{1,0:T(4,128)(4,1)S(1)}, u32[]{:S(2)}) copy-start(pred[1,8]{1,0:T(4,128)(4,1)S(1)} %get-tuple-element.395) | copy-start | bytes 28
  153.4 45.0 %copy-start.49 = (pred[1,8]{1,0:T(4,128)(4,1)}, pred[1,8]{1,0:T(4,128)(4,1)S(1)}, u32[]{:S(2)}) copy-start(pred[1,8]{1,0:T(4,128)(4,1)S(1)} %get-tuple-element.396) | copy-start | bytes 28
  209.5 6.7 copy-start.13
  216.2 6.2 slice-start.4
  216.2 6.2 slice-start.5
  247.0 85.6 %copy-start.25 = (bf16[1024,1024]{1,0:T(8,128)(2,1)S(1)}, bf16[1024,1024]{1,0:T(8,128)(2,1)}, u32[]{:S(2)}) copy-start(bf16[1024,1024]{1,0:T(8,128)(2,1)} %param.29) | copy-start | bytes 6291460
  352.6 11.3 copy-start.12
  352.6 11.3 copy-start.57
  363.9 10.8 copy-start.1
  376.3 4.4 copy-start.21
  377.3 8.1 copy-start.4
  399.6 152.8 %copy-start.30 = (f32[2,16,1,512]{3,2,1,0:T(1,128)S(1)}, f32[2,16,1,512]{3,2,1,0:T(1,128)}, u32[]{:S(2)}) copy-start(f32[2,16,1,512]{3,2,1,0:T(1,128)} %copy-done.29) | copy-start | bytes 196612
  399.6 152.8 %copy-start.33 = (f32[2,512,16]{1,0,2:T(2,128)S(1)}, f32[2,512,16]{1,0,2:T(2,128)}, u32[]{:S(2)}) copy-start(f32[2,512,16]{1,0,2:T(2,128)} %reshape.269) | copy-start | bytes 196612
  399.6 152.8 %copy-start.34 = (f32[2,512,16]{1,0,2:T(2,128)S(1)}, f32[2,512,16]{1,0,2:T(2,128)}, u32[]{:S(2)}) copy-start(f32[2,512,16]{1,0,2:T(2,128)} %neg.17) | copy-start | bytes 196612
  408.5 23.3 %slice-start = ((s8[16777216]{0:T(1024)(128)(4,1)}), s8[4194304]{0:T(1024)(128)(4,1)S(1)}, s32[]{:S(2)}) async-start(s8[16777216]{0:T(1024)(128)(4,1)} %bitcast.292), calls=%async_computation.11 | async-start | bytes 8388608 | tf_op jit(solution)/shard_map/while
  408.5 23.3 %slice-start.1 = ((s8[16777216]{0:T(1024)(128)(4,1)}), s8[4194304]{0:T(1024)(128)(4,1)S(1)}, s32[]{:S(2)}) async-start(s8[16777216]{0:T(1024)(128)(4,1)} %bitcast.292), calls=%async_computation.12 | async-start | bytes 8388608 | tf_op jit(solution)/shard_map/while
  408.5 23.3 %slice-start.2 = ((s8[16777216]{0:T(1024)(128)(4,1)}), s8[4194304]{0:T(1024)(128)(4,1)S(1)}, s32[]{:S(2)}) async-start(s8[16777216]{0:T(1024)(128)(4,1)} %bitcast.292), calls=%async_computation.13 | async-start | bytes 8388608 | tf_op jit(solution)/shard_map/while
  419.3 12.5 %slice-start.3 = ((s8[16777216]{0:T(1024)(128)(4,1)}), s8[4194304]{0:T(1024)(128)(4,1)S(1)}, s32[]{:S(2)}) async-start(s8[16777216]{0:T(1024)(128)(4,1)} %bitcast.292), calls=%async_computation.14 | async-start | bytes 8388608 | tf_op jit(solution)/shard_map/while
  446.6 23.3 %slice-start = ((s8[16777216]{0:T(1024)(128)(4,1)}), s8[4194304]{0:T(1024)(128)(4,1)S(1)}, s32[]{:S(2)}) async-start(s8[16777216]{0:T(1024)(128)(4,1)} %bitcast.292), calls=%async_computation.11 | async-start | bytes 8388608 | tf_op jit(solution)/shard_map/while
  446.6 23.3 %slice-start.1 = ((s8[16777216]{0:T(1024)(128)(4,1)}), s8[4194304]{0:T(1024)(128)(4,1)S(1)}, s32[]{:S(2)}) async-start(s8[16777216]{0:T(1024)(128)(4,1)} %bitcast.292), calls=%async_computation.12 | async-start | bytes 8388608 | tf_op jit(solution)/shard_map/while
  446.6 23.3 %slice-start.2 = ((s8[16777216]{0:T(1024)(128)(4,1)}), s8[4194304]{0:T(1024)(128)(4,1)S(1)}, s32[]{:S(2)}) async-start(s8[16777216]{0:T(1024)(128)(4,1)} %bitcast.292), calls=%async_computation.13 | async-start | bytes 8388608 | tf_op jit(solution)/shard_map/while
  457.4 12.5 %slice-start.3 = ((s8[16777216]{0:T(1024)(128)(4,1)}), s8[4194304]{0:T(1024)(128)(4,1)S(1)}, s32[]{:S(2)}) async-start(s8[16777216]{0:T(1024)(128)(4,1)} %bitcast.292), calls=%async_computation.14 | async-start | bytes 8388608 | tf_op jit(solution)/shard_map/while
  484.7 23.3 %slice-start = ((s8[16777216]{0:T(1024)(128)(4,1)}), s8[4194304]{0:T(1024)(128)(4,1)S(1)}, s32[]{:S(2)}) async-start(s8[16777216]{0:T(1024)(128)(4,1)} %bitcast.292), calls=%async_computation.11 | async-start | bytes 8388608 | tf_op jit(solution)/shard_map/while
  484.7 23.3 %slice-start.1 = ((s8[16777216]{0:T(1024)(128)(4,1)}), s8[4194304]{0:T(1024)(128)(4,1)S(1)}, s32[]{:S(2)}) async-start(s8[16777216]{0:T(1024)(128)(4,1)} %bitcast.292), calls=%async_computation.12 | async-start | bytes 8388608 | tf_op jit(solution)/shard_map/while
  484.7 23.3 %slice-start.2 = ((s8[16777216]{0:T(1024)(128)(4,1)}), s8[4194304]{0:T(1024)(128)(4,1)S(1)}, s32[]{:S(2)}) async-start(s8[16777216]{0:T(1024)(128)(4,1)} %bitcast.292), calls=%async_computation.13 | async-start | bytes 8388608 | tf_op jit(solution)/shard_map/while
  495.5 12.5 %slice-start.3 = ((s8[16777216]{0:T(1024)(128)(4,1)}), s8[4194304]{0:T(1024)(128)(4,1)S(1)}, s32[]{:S(2)}) async-start(s8[16777216]{0:T(1024)(128)(4,1)} %bitcast.292), calls=%async_computation.14 | async-start | bytes 8388608 | tf_op jit(solution)/shard_map/while
  522.8 23.3 %slice-start = ((s8[16777216]{0:T(1024)(128)(4,1)}), s8[4194304]{0:T(1024)(128)(4,1)S(1)}, s32[]{:S(2)}) async-start(s8[16777216]{0:T(1024)(128)(4,1)} %bitcast.292), calls=%async_computation.11 | async-start | bytes 8388608 | tf_op jit(solution)/shard_map/while
  522.8 23.3 %slice-start.1 = ((s8[16777216]{0:T(1024)(128)(4,1)}), s8[4194304]{0:T(1024)(128)(4,1)S(1)}, s32[]{:S(2)}) async-start(s8[16777216]{0:T(1024)(128)(4,1)} %bitcast.292), calls=%async_computation.12 | async-start | bytes 8388608 | tf_op jit(solution)/shard_map/while
  522.8 23.3 %slice-start.2 = ((s8[16777216]{0:T(1024)(128)(4,1)}), s8[4194304]{0:T(1024)(128)(4,1)S(1)}, s32[]{:S(2)}) async-start(s8[16777216]{0:T(1024)(128)(4,1)} %bitcast.292), calls=%async_computation.13 | async-start | bytes 8388608 | tf_op jit(solution)/shard_map/while
  533.6 12.5 %slice-start.3 = ((s8[16777216]{0:T(1024)(128)(4,1)}), s8[4194304]{0:T(1024)(128)(4,1)S(1)}, s32[]{:S(2)}) async-start(s8[16777216]{0:T(1024)(128)(4,1)} %bitcast.292), calls=%async_computation.14 | async-start | bytes 8388608 | tf_op jit(solution)/shard_map/while
  558.8 8.0 copy-start.37
  587.8 421.5 %reduce-scatter.5.cloned.1.call-start = ((), (), s32[]{:S(2)}) async-start(), calls=%async_computation.8 | async-start | bytes 25067520 | tf_op jit(solution)/shard_map/reduce_scatter | solution.py:326
  609.5 23.4 %copy-start.22 = (bf16[1024,1024]{0,1:T(8,128)(2,1)S(1)}, bf16[1024,1024]{0,1:T(8,128)(2,1)}, u32[]{:S(2)}) copy-start(bf16[1024,1024]{0,1:T(8,128)(2,1)} %fusion.75) | copy-start | bytes 6291460
  653.5 8.4 copy-start.46
  662.1 8.1 copy-start.8
  682.3 19.6 %copy-start.32 = (bf16[1024,16,16]{0,2,1:T(8,128)(2,1)S(1)}, bf16[1024,16,16]{0,2,1:T(8,128)(2,1)}, u32[]{:S(2)}) copy-start(bf16[1024,16,16]{0,2,1:T(8,128)(2,1)} %copy-done.31) | copy-start | bytes 1572868
  682.3 19.6 %copy-start.45 = (bf16[273]{0:T(512)(128)(2,1)S(1)}, bf16[273]{0:T(512)(128)(2,1)}, u32[]{:S(2)}) copy-start(bf16[273]{0:T(512)(128)(2,1)} %copy-done.44) | copy-start | bytes 1642
  701.9 8.7 copy-start.15
  713.6 6.5 copy-start.10
  720.1 12.1 %copy-start.28 = (f32[4,1024,4,16]{1,3,2,0:T(8,128)S(1)}, f32[4,1024,4,16]{1,3,2,0:T(8,128)}, u32[]{:S(2)}) copy-start(f32[4,1024,4,16]{1,3,2,0:T(8,128)} %get-tuple-element.230) | copy-start | bytes 3145732
  737.3 6.1 copy-start.58
  791.0 329.0 %all-gather.22.cloned.1.call-start = ((), (), s32[]{:S(2)}) async-start(), calls=%async_computation.9 | async-start | bytes 13926400 | tf_op jit(solution)/shard_map/all_gather | solution.py:342
  1133.1 5.9 copy-start.18
  (24 other events, 49.9 us)
Sparse Core Ops, SparseCore 0:
  9.6 36.0 all-gather.11
  65.8 57.8 all-gather.23
  125.3 27.8 all-gather.13
  154.7 59.1 all-gather.15
  215.3 57.9 all-gather.17
  274.7 57.9 all-gather.19
  588.0 69.0 reduce-scatter.2
  791.2 218.1 reduce-scatter.4
  1011.2 108.8 all-gather.21
